TPU v7x, 128 devices: a whole 4x4x4 slice. The times are simulated.
128 devices in a mesh: row: 16 (over x, z), col: 8 (over y, core).
Axes of the slice: x: 4, y: 4, z: 4, core: 2. Of those that a mesh axis runs over, the one named last changes fastest.
Arguments:
- hole_panel: bfloat16 [8192, 98304], P('row', 'col'), may hold values from -0.0546875 to 0.0546875
- amplitudes: bfloat16 [768, 98304], P(('row', 'col')), may hold values from -6 to 6
- row_sizes: int32 [8], replicated, may hold values from 1 to 2048, 8192 in all
- col_sizes: int32 [8], replicated, may hold values from 1 to 24576, 98304 in all
- pair_order: int32 [768], replicated, may hold values from 0 to 767, each once
Outputs:
- cycle_term: float32 [8192, 768], P('row', 'col')
Inputs may be any that keep to these rules, and one draw needn't show every extreme that they name: `row_sizes`: the rows of irrep g follow those of the irreps below g; the sizes sum to 8192, the largest is 2048. `col_sizes`: the indices of irrep g follow those of the irreps below g; the sizes sum to 98304, the largest is 24576. `pair_order`: each pair appears once.
All inputs are finite; a program needn't handle non-finite values.
Results may differ from a plain program's by a relative error of at most 0.0003.
Values may be sent and summed in bfloat16 or wider, within the bound.
No kernel may reach another device: no remote copies, remote signals or barrier semaphores. Data moves between devices by JAX's collectives and lax.ppermute only.
A program may use at most 192 MiB of HBM per device.

v0:
```python
import jax
import jax.numpy as jnp
from jax import lax
from jax.sharding import PartitionSpec as P


def irrep_labels(sizes, count, offset):
    position = offset + lax.iota(jnp.int32, count)
    bounds = jnp.cumsum(sizes)
    return jnp.sum((position[:, None] >= bounds[None, :]).astype(jnp.int32), axis=1)


def contract(masked, piece):
    numbers = (((1,), (1,)), ((), ()))
    return lax.dot_general(masked, piece, numbers, preferred_element_type=jnp.float32)


def on_device(hole_panel, amplitudes, row_sizes, col_sizes, pair_order):
    row_count, col_count = hole_panel.shape
    row_devices = lax.axis_size("row")
    col_devices = lax.axis_size("col")
    per_device = amplitudes.shape[0]
    pair_total = per_device * row_devices * col_devices
    row_irrep = irrep_labels(row_sizes, row_count, lax.axis_index("row") * row_count)
    col_irrep = irrep_labels(col_sizes, col_count, lax.axis_index("col") * col_count)
    masked = jnp.where(
        row_irrep[:, None] == col_irrep[None, :], hole_panel, jnp.zeros((), hole_panel.dtype)
    )
    split_rows = lax.all_to_all(amplitudes, "col", split_axis=1, concat_axis=0, tiled=True)
    stored = contract(masked, lax.all_gather(split_rows, "row", axis=0, tiled=True))
    logical = jnp.zeros((row_count, pair_total), jnp.float32).at[:, pair_order].set(stored)
    return lax.psum_scatter(logical, "col", scatter_dimension=1, tiled=True)


def solution(mesh):
    in_specs = (P("row", "col"), P(("row", "col"), None), P(), P(), P())
    out_specs = P("row", "col")
    return jax.shard_map(
        on_device, mesh=mesh, in_specs=in_specs, out_specs=out_specs, check_vma=False
    )
```

profile of v0, /device:TPU:0, one launch (start us, length us, event | category | flops | bytes accessed | tf_op | source)
XLA Modules:
  0.0 221.0 jit_solution(13136093127057807586)
XLA Ops:
  6.5 0.0 all-gather.2.cloned.1.call-start
  6.5 26.4 %all_to_all.19 = bf16[6,8,12288]{2,0,1:T(8,128)(2,1)S(1)} all-to-all(bf16[6,8,12288]{2,0,1:T(8,128)(2,1)} %bitcast.10), channel_id=1, replica_groups=mesh['row'=16,'col'=8] {'col'}, dimensions={1} | all-to-all | bytes 2359296 | tf_op jit(solution)/shard_map/all_to_all | solution.py:29
  32.9 0.0 copy-start.1
  32.9 0.0 copy-start.2
  32.9 0.0 copy-start
  32.9 1.3 all_to_all.17
  34.2 0.0 all-gather.2.cloned.1.call-update
  34.2 0.0 reduce-scatter.2.cloned.1.call-start
  34.3 0.0 copy-done.1
  34.3 0.2 reduce-window.17
  34.5 0.0 copy-done.2
  34.5 0.2 reduce-window.16
  34.7 0.1 convert_reduce_fusion.1
  34.8 0.2 convert_reduce_fusion
  34.9 0.0 copy-done
  35.0 121.9 %all-gather.2.cloned.1.call-done = bf16[768,12288]{1,0:T(8,128)(2,1)} async-done(((bf16[48,12288]{1,0:T(8,128)(2,1)}), bf16[768,12288]{1,0:T(8,128)(2,1)}) %all-gather.2.cloned.1.call-update) | async-done | bytes 18874384 | tf_op jit(solution)/shard_map/all_gather | solution.py:30
  156.9 17.6 %fusion.4 = f32[768,512]{0,1:T(8,128)S(1)} fusion(bf16[768,12288]{1,0:T(8,128)(2,1)} %all-gather.2.cloned.1.call-done, bf16[512,12288]{1,0:T(8,128)(2,1)} %param.5, s32[12288]{0:T(1024)S(1)} %convert_reduce_fusion, s32[512]{0:T(512)S(1)} %convert_reduce_fusion.1), kind=kOutput, calls=%fused_computation.6 | convolution fusion | flops 9676259328 | bytes 33081344 | tf_op jit(solution)/shard_map/dot_general | solution.py:15
  174.5 0.5 copy.10
  175.0 6.7 %scatter_custom_fusion = f32[512,768]{0,1:T(8,128)} fusion(s32[768]{0:T(1024)S(1)} %compare_select_fusion.4, f32[768,512]{1,0:T(8,128)S(1)} %copy.10, f32[]{:T(128)} %constant.9.clone.1), kind=kCustom, calls=%fused_computation.7 | custom fusion | bytes 1572868 | tf_op jit(solution)/shard_map/scatter | solution.py:31
  181.7 0.0 reduce-scatter.2.cloned.1.call-update
  181.7 32.5 %reduce-scatter.2.cloned.1.call-done = f32[512,96]{0,1:T(8,128)} async-done(((f32[512,768]{0,1:T(8,128)}), f32[512,96]{0,1:T(8,128)}) %reduce-scatter.2.cloned.1.call-update) | async-done | bytes 196624 | tf_op jit(solution)/shard_map/reduce_scatter | solution.py:32
  (3 shorter events, 0.0 us)
Async XLA Ops:
  6.5 150.3 %all-gather.2.cloned.1.call-start = ((), (), s32[]{:S(2)}) async-start(), calls=%async_computation.2 | async-start | bytes 20054016 | tf_op jit(solution)/shard_map/all_gather | solution.py:30
  32.9 1.4 copy-start.1
  32.9 1.6 copy-start.2
  32.9 2.1 copy-start
  34.2 180.0 %reduce-scatter.2.cloned.1.call-start = ((), (), s32[]{:S(2)}) async-start(), calls=%async_computation.3 | async-start | bytes 1769472 | tf_op jit(solution)/shard_map/reduce_scatter | solution.py:32
Sparse Core Ops, SparseCore 0:
  34.3 122.4 all-gather.1
  181.9 32.3 reduce-scatter.1
where the time goes:
time: 221 us
  waiting for transfers between devices  154 us (70%)
  blocking collectives  26.4 us (12%)
  matrix products  17.6 us (8%)
  between operations  13.5 us (6%)
  local copies, waits for them, and re-layouts  8.5 us (4%)
    all_gather x1, waiting for transfers between devices, on_device(): lax.all_gather(split_rows, 'row', axis=0, tiled=True)  122 us
    reduce_scatter x1, waiting for transfers between devices, on_device(): return lax.psum_scatter(logical, 'col', scatter_dimension=1, tiled=True)  32.5 us
    all_to_all x1, blocking collectives, on_device(): lax.all_to_all(amplitudes, 'col', split_axis=1, concat_axis=0, tiled=True)  26.4 us
    dot_general x1, matrix products, contract(): lax.dot_general(masked, piece, numbers, preferred_element_type=jnp.float32)  17.6 us
    scatter x1, local copies, waits for them, and re-layouts, on_device(): jnp.zeros((row_count, pair_total), jnp.float32).at[:, pair_order]  6.72 us
  transfers between devices with their start and end apart: 2, of which 2 were waited for; matrix products, arithmetic and copies ran while one was open for 0% of the time, Pallas kernels for 0%

commit v1 on v0

--- a/solution.py
+++ b/solution.py
@@ -27,7 +27,12 @@
         row_irrep[:, None] == col_irrep[None, :], hole_panel, jnp.zeros((), hole_panel.dtype)
     )
     split_rows = lax.all_to_all(amplitudes, "col", split_axis=1, concat_axis=0, tiled=True)
-    stored = contract(masked, lax.all_gather(split_rows, "row", axis=0, tiled=True))
+    stored = contract(
+        masked,
+        jnp.concatenate(
+            lax.all_to_all(jnp.stack([split_rows] * lax.axis_size("row")), "row", 0, 0), axis=0
+        ),
+    )
     logical = jnp.zeros((row_count, pair_total), jnp.float32).at[:, pair_order].set(stored)
     return lax.psum_scatter(logical, "col", scatter_dimension=1, tiled=True)
 

time: 221 us -> 450 us (2.04)
  waiting for transfers between devices: 154 us -> 370 us
  starting transfers between devices: 0.04 us -> 8.1 us
  local copies, waits for them, and re-layouts: 8.5 us -> 14.4 us
    all_to_all x0 -> x1, waiting for transfers between devices: none -> 331 us  [on_device(): lax.all_to_all(jnp.stack([split_rows] * lax.axis_size('row')), 'row', 0, 0)]
    all_gather x1 -> x0, waiting for transfers between devices: 122 us -> none  [on_device(): lax.all_gather(split_rows, 'row', axis=0, tiled=True)]
    all_to_all x0 -> x1, starting transfers between devices: none -> 8.05 us  [on_device(): lax.all_to_all(jnp.stack([split_rows] * lax.axis_size('row')), 'row', 0, 0)]
    another operation x0 -> x2, local copies, waits for them, and re-layouts: none -> 7.22 us  [on_device(): jnp.stack([split_rows] * lax.axis_size('row'))]
    reduce_scatter x1, waiting for transfers between devices: 32.5 us -> 38.3 us  [on_device(): return lax.psum_scatter(logical, 'col', scatter_dimension=1, tiled=True)]
where the time goes in v1:
time: 450 us
  waiting for transfers between devices  370 us (82%)
  blocking collectives  26.4 us (6%)
  matrix products  17.6 us (4%)
  local copies, waits for them, and re-layouts  14.4 us (3%)
  between operations  13.5 us (3%)
  starting transfers between devices  8.1 us (2%)
    all_to_all x1, waiting for transfers between devices, on_device(): lax.all_to_all(jnp.stack([split_rows] * lax.axis_size('row')), 'row', 0, 0)  331 us
    reduce_scatter x1, waiting for transfers between devices, on_device(): return lax.psum_scatter(logical, 'col', scatter_dimension=1, tiled=True)  38.3 us
    all_to_all x1, blocking collectives, on_device(): lax.all_to_all(amplitudes, 'col', split_axis=1, concat_axis=0, tiled=True)  26.4 us
    dot_general x1, matrix products, contract(): lax.dot_general(masked, piece, numbers, preferred_element_type=jnp.float32)  17.6 us
  transfers between devices with their start and end apart: 2, of which 2 were waited for; matrix products, arithmetic and copies ran while one was open for 0% of the time, Pallas kernels for 0%

profile of v1, /device:TPU:0, one launch (start us, length us, event | category | flops | bytes accessed | tf_op | source)
XLA Modules:
  0.0 450.2 jit_solution(3165990990676124405)
XLA Ops:
  6.5 26.4 %all_to_all.21 = bf16[6,8,12288]{2,0,1:T(8,128)(2,1)S(1)} all-to-all(bf16[6,8,12288]{2,0,1:T(8,128)(2,1)} %bitcast.11), channel_id=1, replica_groups=mesh['row'=16,'col'=8] {'col'}, dimensions={1} | all-to-all | bytes 2359296 | tf_op jit(solution)/shard_map/all_to_all | solution.py:29
  32.9 0.5 stack.4
  33.4 6.8 %stack.5 = bf16[16,48,12288]{2,1,0:T(8,128)(2,1)} broadcast(bf16[48,12288]{1,0:T(8,128)(2,1)S(1)} %stack.4), dimensions={1,2} | broadcast | bytes 20054016 | tf_op jit(solution)/shard_map/stack | solution.py:33
  40.1 0.0 copy-start.1
  40.1 0.0 copy-start.2
  40.1 0.0 copy-start
  40.1 8.1 %all-to-all-start.1 = ((bf16[16,48,12288]{2,1,0:T(8,128)(2,1)}), bf16[16,48,12288]{2,1,0:T(8,128)(2,1)}, u32[]{:S(2)}, u32[]{:S(2)}) async-start(bf16[16,48,12288]{2,1,0:T(8,128)(2,1)} %stack.5), calls=%async_computation.1 | async-start | bytes 37748736 | tf_op jit(solution)/shard_map/all_to_all | solution.py:33
  48.2 0.0 reduce-scatter.2.cloned.1.call-start
  48.2 0.0 copy-done.1
  48.3 0.2 reduce-window.17
  48.4 0.0 copy-done.2
  48.4 0.2 reduce-window.16
  48.6 0.1 convert_reduce_fusion.1
  48.7 0.2 convert_reduce_fusion
  48.9 0.0 copy-done
  48.9 331.2 %all-to-all-done.1 = bf16[16,48,12288]{2,1,0:T(8,128)(2,1)} async-done(((bf16[16,48,12288]{2,1,0:T(8,128)(2,1)}), bf16[16,48,12288]{2,1,0:T(8,128)(2,1)}, u32[]{:S(2)}, u32[]{:S(2)}) %all-to-all-start.1) | async-done | bytes 18874400 | tf_op jit(solution)/shard_map/all_to_all | solution.py:33
  380.2 17.6 %fusion.4 = f32[768,512]{0,1:T(8,128)S(1)} fusion(bf16[768,12288]{1,0:T(8,128)(2,1)} %bitcast.6, bf16[512,12288]{1,0:T(8,128)(2,1)} %param.5, s32[12288]{0:T(1024)S(1)} %convert_reduce_fusion, s32[512]{0:T(512)S(1)} %convert_reduce_fusion.1), kind=kOutput, calls=%fused_computation.6 | convolution fusion | flops 9676259328 | bytes 33081344 | tf_op jit(solution)/shard_map/dot_general | solution.py:15
  397.8 0.5 copy.10
  398.3 6.7 %scatter_custom_fusion = f32[512,768]{0,1:T(8,128)} fusion(s32[768]{0:T(1024)S(1)} %compare_select_fusion.4, f32[768,512]{1,0:T(8,128)S(1)} %copy.10, f32[]{:T(128)} %constant.9.clone.1), kind=kCustom, calls=%fused_computation.7 | custom fusion | bytes 1572868 | tf_op jit(solution)/shard_map/scatter | solution.py:36
  405.0 0.0 reduce-scatter.2.cloned.1.call-update
  405.0 38.3 %reduce-scatter.2.cloned.1.call-done = f32[512,96]{0,1:T(8,128)} async-done(((f32[512,768]{0,1:T(8,128)}), f32[512,96]{0,1:T(8,128)}) %reduce-scatter.2.cloned.1.call-update) | async-done | bytes 196624 | tf_op jit(solution)/shard_map/reduce_scatter | solution.py:37
  (3 shorter events, 0.0 us)
Async XLA Ops:
  40.1 8.1 %copy-start.1 = (s32[8]{0:T(128)S(1)}, s32[8]{0:T(128)}, u32[]{:S(2)}) copy-start(s32[8]{0:T(128)} %param.8) | copy-start | bytes 100
  40.1 8.3 %copy-start.2 = (s32[8]{0:T(128)S(1)}, s32[8]{0:T(128)}, u32[]{:S(2)}) copy-start(s32[8]{0:T(128)} %param.7) | copy-start | bytes 100
  40.1 8.8 %copy-start = (s32[768]{0:T(1024)S(1)}, s32[768]{0:T(1024)}, u32[]{:S(2)}) copy-start(s32[768]{0:T(1024)} %param.9) | copy-start | bytes 9220
  40.1 340.1 %all-to-all-start.1 = ((bf16[16,48,12288]{2,1,0:T(8,128)(2,1)}), bf16[16,48,12288]{2,1,0:T(8,128)(2,1)}, u32[]{:S(2)}, u32[]{:S(2)}) async-start(bf16[16,48,12288]{2,1,0:T(8,128)(2,1)} %stack.5), calls=%async_computation.1 | async-start | bytes 37748736 | tf_op jit(solution)/shard_map/all_to_all | solution.py:33
  48.2 395.2 %reduce-scatter.2.cloned.1.call-start = ((), (), s32[]{:S(2)}) async-start(), calls=%async_computation.3 | async-start | bytes 1769472 | tf_op jit(solution)/shard_map/reduce_scatter | solution.py:37
Sparse Core Ops, SparseCore 0:
  405.2 38.1 reduce-scatter.1

commit v2 on v0

--- a/solution.py
+++ b/solution.py
@@ -26,7 +26,10 @@
     masked = jnp.where(
         row_irrep[:, None] == col_irrep[None, :], hole_panel, jnp.zeros((), hole_panel.dtype)
     )
-    split_rows = lax.all_to_all(amplitudes, "col", split_axis=1, concat_axis=0, tiled=True)
+    split_rows = jnp.concatenate(
+        lax.all_to_all(jnp.stack(jnp.split(amplitudes, lax.axis_size("col"), axis=1)), "col", 0, 0),
+        axis=0,
+    )
     stored = contract(masked, lax.all_gather(split_rows, "row", axis=0, tiled=True))
     logical = jnp.zeros((row_count, pair_total), jnp.float32).at[:, pair_order].set(stored)
     return lax.psum_scatter(logical, "col", scatter_dimension=1, tiled=True)

time: 221 us -> 228 us (1.032)
  local copies, waits for them, and re-layouts: 8.5 us -> 15.6 us
    unnamed x6 -> x13, local copies, waits for them, and re-layouts: 0.01 us -> 6.61 us
where the time goes in v2:
time: 228 us
  waiting for transfers between devices  154 us (68%)
  blocking collectives  26.2 us (11%)
  matrix products  17.6 us (8%)
  local copies, waits for them, and re-layouts  15.6 us (7%)
  between operations  13.5 us (6%)
    all_gather x1, waiting for transfers between devices, on_device(): lax.all_gather(split_rows, 'row', axis=0, tiled=True)  122 us
    reduce_scatter x1, waiting for transfers between devices, on_device(): return lax.psum_scatter(logical, 'col', scatter_dimension=1, tiled=True)  32.5 us
    all_to_all x1, blocking collectives, on_device(): lax.all_to_all(jnp.stack(jnp.split(amplitudes, lax.axis_size('col'), axis...  26.2 us
    dot_general x1, matrix products, contract(): lax.dot_general(masked, piece, numbers, preferred_element_type=jnp.float32)  17.6 us
    scatter x1, local copies, waits for them, and re-layouts, on_device(): jnp.zeros((row_count, pair_total), jnp.float32).at[:, pair_order]  6.72 us
    unnamed x13, local copies, waits for them, and re-layouts  6.61 us
  transfers between devices with their start and end apart: 2, of which 2 were waited for; matrix products, arithmetic and copies ran while one was open for 0% of the time, Pallas kernels for 0%

profile of v2, /device:TPU:0, one launch (start us, length us, event | category | flops | bytes accessed | tf_op | source)
XLA Modules:
  0.0 228.0 jit_solution(15427910160815590159)
XLA Ops:
  6.5 0.0 all-gather.2.cloned.1.call-start
  6.5 0.9 bitcast_dynamic-update-slice_fusion.7
  7.5 0.9 bitcast_dynamic-update-slice_fusion.6
  8.4 0.9 bitcast_dynamic-update-slice_fusion.5
  9.4 0.9 bitcast_dynamic-update-slice_fusion.4
  10.3 0.9 bitcast_dynamic-update-slice_fusion.3
  11.3 0.9 bitcast_dynamic-update-slice_fusion.2
  12.2 0.9 bitcast_dynamic-update-slice_fusion.1
  13.2 0.9 bitcast_dynamic-update-slice_fusion
  14.1 26.2 %all_to_all.5 = bf16[8,6,12288]{2,1,0:T(8,128)(2,1)S(1)} all-to-all(bf16[8,6,12288]{2,1,0:T(8,128)(2,1)S(1)} %bitcast_dynamic-update-slice_fusion), channel_id=1, replica_groups=mesh['row'=16,'col'=8] {'col'}, dimensions={0} | all-to-all | bytes 2359296 | tf_op jit(solution)/shard_map/all_to_all | solution.py:30
  40.3 0.0 copy-start.1
  40.3 0.0 copy-start.2
  40.3 0.0 copy-start
  40.3 1.3 reshape.65
  41.6 0.0 all-gather.2.cloned.1.call-update
  41.6 0.0 reduce-scatter.2.cloned.1.call-start
  41.6 0.0 copy-done.1
  41.7 0.2 reduce-window.17
  41.8 0.0 copy-done.2
  41.8 0.2 reduce-window.16
  42.0 0.1 convert_reduce_fusion.1
  42.1 0.2 convert_reduce_fusion
  42.3 0.0 copy-done
  42.3 121.9 %all-gather.2.cloned.1.call-done = bf16[768,12288]{1,0:T(8,128)(2,1)} async-done(((bf16[48,12288]{1,0:T(8,128)(2,1)}), bf16[768,12288]{1,0:T(8,128)(2,1)}) %all-gather.2.cloned.1.call-update) | async-done | bytes 18874384 | tf_op jit(solution)/shard_map/all_gather | solution.py:33
  164.3 17.6 %fusion = f32[768,512]{1,0:T(8,128)S(1)} fusion(bf16[768,12288]{1,0:T(8,128)(2,1)} %all-gather.2.cloned.1.call-done, bf16[512,12288]{1,0:T(8,128)(2,1)} %param.5, s32[12288]{0:T(1024)S(1)} %convert_reduce_fusion, s32[512]{0:T(512)S(1)} %convert_reduce_fusion.1), kind=kOutput, calls=%fused_computation.2 | convolution fusion | flops 9676259328 | bytes 33081344 | tf_op jit(solution)/shard_map/dot_general | solution.py:15
  181.9 6.7 %scatter_custom_fusion = f32[512,768]{0,1:T(8,128)} fusion(s32[768]{0:T(1024)S(1)} %compare_select_fusion.2, f32[768,512]{1,0:T(8,128)S(1)} %fusion, f32[]{:T(128)} %constant.9.clone.1), kind=kCustom, calls=%fused_computation.6 | custom fusion | bytes 1572868 | tf_op jit(solution)/shard_map/scatter | solution.py:34
  188.6 0.0 reduce-scatter.2.cloned.1.call-update
  188.6 32.5 %reduce-scatter.2.cloned.1.call-done = f32[512,96]{0,1:T(8,128)} async-done(((f32[512,768]{0,1:T(8,128)}), f32[512,96]{0,1:T(8,128)}) %reduce-scatter.2.cloned.1.call-update) | async-done | bytes 196624 | tf_op jit(solution)/shard_map/reduce_scatter | solution.py:35
  (3 shorter events, 0.0 us)
Async XLA Ops:
  6.5 157.7 %all-gather.2.cloned.1.call-start = ((), (), s32[]{:S(2)}) async-start(), calls=%async_computation.2 | async-start | bytes 20054016 | tf_op jit(solution)/shard_map/all_gather | solution.py:33
  40.3 1.4 copy-start.1
  40.3 1.6 copy-start.2
  40.3 2.1 copy-start
  41.6 179.5 %reduce-scatter.2.cloned.1.call-start = ((), (), s32[]{:S(2)}) async-start(), calls=%async_computation.3 | async-start | bytes 1769472 | tf_op jit(solution)/shard_map/reduce_scatter | solution.py:35
Sparse Core Ops, SparseCore 0:
  41.7 122.4 all-gather.1
  188.7 32.3 reduce-scatter.1
